TPU v7x, 32 devices: a whole 2x2x4 slice. The times are simulated.
32 devices in a mesh: tok: 8 (over z, x), tp: 4 (over y, core).
Axes of the slice: x: 2, y: 2, z: 4, core: 2. Of those that a mesh axis runs over, the one named last changes fastest.
Arguments:
- resid: bfloat16 [1024, 8192], P('tok', 'tp'), may hold values from -7 to 7
- norm_gain: float32 [8192], P('tp'), may hold values from 0.5 to 1.5
- head_in: bfloat16 [8192, 2048], P('tp'), may hold values from -0.088388348 to 0.088388348
- head_bias: float32 [2048], replicated, may hold values from -3 to 3
- head_out: float32 [16, 128], replicated, may hold values from -0.26516504 to 0.26516504
- targets: float32 [1024, 16], P('tok'), may hold values from -12 to 12
- label_mask: int32 [1024, 16], P('tok'), may hold values 0 or 1
- obj_weight: int32 [16], replicated, may hold values from 1 to 16
Outputs:
- resid_grad: bfloat16 [1024, 8192], P('tok', 'tp')
- gain_grad: float32 [8192], P('tp')
- head_in_grad: float32 [8192, 2048], P('tp', 'tok')
- head_bias_grad: float32 [2048], replicated
All inputs are finite; a program needn't handle non-finite values. No bound on the sum of `label_mask` on one device may be relied on, other than what follows from the above.
Results may differ from a plain program's by a relative error of at most 0.0078.
Values may be sent and summed in bfloat16 or wider, within the bound.
No kernel may reach another device: no remote copies, remote signals or barrier semaphores. Data moves between devices by JAX's collectives and lax.ppermute only.
A program may use at most 128 MiB of HBM per device.

v0:
```python
import jax
import jax.numpy as jnp
from jax import lax
from jax.sharding import PartitionSpec as P

D = 8192
norm_eps = 1e-05
grad_eps = 1e-06
denominator = 8.0


def head_gradient(preact, head_out, targets, label_mask):
    count = preact.shape[0]
    objectives, hidden = head_out.shape
    cube = preact.reshape(count, objectives, hidden)
    squash = jax.nn.sigmoid(cube)
    scores = jnp.sum(cube * squash * head_out[None], axis=2)
    errors = label_mask.astype(jnp.float32) * (scores - targets)
    slopes = squash * (1.0 + cube * (1.0 - squash))
    row_grad = (errors[:, :, None] * head_out[None] * slopes).astype(jnp.bfloat16)
    return row_grad.reshape(count, objectives * hidden)


def per_device(resid, norm_gain, head_in, head_bias, head_out, targets, label_mask, obj_weight):
    tok_rows = resid.shape[0]
    objectives, hidden = head_out.shape
    total_tokens = tok_rows * lax.axis_size("tok")
    floated = resid.astype(jnp.float32)
    row_sums = lax.psum(jnp.sum(floated * floated, axis=1), "tp")
    inverse = lax.rsqrt(row_sums[:, None] / D + norm_eps)
    unit = floated * inverse
    normed = (unit * norm_gain[None, :]).astype(jnp.bfloat16)
    partial_value = jnp.dot(normed, head_in, preferred_element_type=jnp.float32)
    quarter = lax.psum_scatter(partial_value, "tp", scatter_dimension=0, tiled=True)
    share = quarter.shape[0]
    offset = lax.axis_index("tp") * share
    part_targets = lax.dynamic_slice_in_dim(targets, offset, share, 0)
    part_mask = lax.dynamic_slice_in_dim(label_mask, offset, share, 0)
    part_grad = head_gradient(quarter + head_bias[None, :], head_out, part_targets, part_mask)
    row_grad = lax.all_gather(part_grad, "tp", axis=0, tiled=True)
    grad_float = row_grad.astype(jnp.float32)

    def objective_square(which):
        grad_slice = lax.dynamic_slice_in_dim(row_grad, which * hidden, hidden, 1)
        weight_slice = lax.dynamic_slice_in_dim(head_in, which * hidden, hidden, 1)
        feature_grad = lax.dot_general(
            grad_slice, weight_slice, (((1,), (1,)), ((), ())), preferred_element_type=jnp.float32
        )
        return jnp.sum(feature_grad * feature_grad)

    local_squares = lax.map(objective_square, jnp.arange(objectives))
    squares = lax.psum(local_squares, ("tok", "tp"))
    obj_rms = jnp.sqrt(squares / (total_tokens * D) + grad_eps)
    balance = obj_weight.astype(jnp.float32) / denominator / obj_rms
    balance_cols = jnp.repeat(balance, hidden)
    pre_grad = (grad_float * balance_cols[None, :]).astype(jnp.bfloat16)
    norm_grad = lax.dot_general(
        pre_grad, head_in, (((1,), (1,)), ((), ())), preferred_element_type=jnp.float32
    )
    gain_sum, bias_sum = lax.psum(
        (jnp.sum(norm_grad * unit, axis=0), jnp.sum(grad_float, axis=0)), "tok"
    )
    gain_grad = gain_sum / total_tokens
    head_bias_grad = bias_sum * balance_cols / total_tokens
    projection = lax.psum(jnp.sum(unit * norm_gain[None, :] * norm_grad, axis=1), "tp")
    resid_grad = (
        inverse * (norm_gain[None, :] * norm_grad - unit * (projection[:, None] / D))
    ).astype(jnp.bfloat16)
    weight_term = lax.dot_general(
        normed, row_grad, (((0,), (0,)), ((), ())), preferred_element_type=jnp.float32
    )
    summed_block = lax.psum_scatter(weight_term, "tok", scatter_dimension=1, tiled=True)
    columns = summed_block.shape[1]
    col_scale = lax.dynamic_slice_in_dim(balance_cols, lax.axis_index("tok") * columns, columns, 0)
    head_in_grad = summed_block * col_scale[None, :] / total_tokens
    return (resid_grad, gain_grad, head_in_grad, head_bias_grad)


def solution(mesh):
    return jax.shard_map(
        per_device,
        mesh=mesh,
        in_specs=(
            P("tok", "tp"),
            P("tp"),
            P("tp", None),
            P(),
            P(),
            P("tok", None),
            P("tok", None),
            P(),
        ),
        out_specs=(P("tok", "tp"), P("tp"), P("tp", "tok"), P()),
        check_vma=False,
    )
```

profile of v0, /device:TPU:0, one launch (start us, length us, event | category | flops | bytes accessed | tf_op | source)
XLA Modules:
  0.0 359.1 jit_solution(12255660014555638462)
XLA Ops:
  7.2 1.2 fusion.14
  8.5 8.4 %psum.35 = f32[128]{0:T(128)S(1)} all-reduce(f32[128]{0:T(128)S(1)} %fusion.14), channel_id=1, replica_groups=mesh['tok'=8,'tp'=4] {'tp'}, use_global_device_ids=true, to_apply=%region_1.0 | all-reduce | flops 128 | bytes 1024 | tf_op jit(solution)/shard_map/psum | solution.py:29
  16.9 5.9 %fusion.26 = f32[128,2048]{1,0:T(8,128)} fusion(bf16[2048,2048]{1,0:T(8,128)(2,1)} %param.12, bf16[128,2048]{1,0:T(8,128)(2,1)} %param.10, f32[2048]{0:T(1024)} %param.11, f32[128]{0:T(128)S(1)} %add_rsqrt_fusion), kind=kOutput, calls=%fused_computation.35 | convolution fusion | flops 1074790400 | bytes 9970176 | tf_op jit(solution)/shard_map/dot_general | solution.py:33
  23.2 24.9 %reduce-scatter.3.cloned.1.call-done = f32[32,2048]{1,0:T(8,128)} async-done(((f32[128,2048]{1,0:T(8,128)}), f32[32,2048]{1,0:T(8,128)}) %reduce-scatter.3.cloned.1.call-update) | async-done | bytes 262160 | tf_op jit(solution)/shard_map/reduce_scatter | solution.py:34
  48.1 1.0 add_bitcast_fusion
  49.5 1.1 fusion.20
  50.6 6.6 %all_gather.3 = bf16[128,2048]{1,0:T(8,128)(2,1)S(1)} all-gather(bf16[32,2048]{1,0:T(8,128)(2,1)S(1)} %fusion.20), channel_id=1, replica_groups=mesh['tok'=8,'tp'=4] {'tp'}, dimensions={0}, use_global_device_ids=true | all-gather | bytes 655360 | tf_op jit(solution)/shard_map/all_gather | solution.py:40
  57.3 8.2 %fusion.24 = f32[2048,2048]{1,0:T(8,128)} fusion(bf16[128,2048]{1,0:T(8,128)(2,1)S(1)} %all_gather.3, bf16[128,2048]{1,0:T(8,128)(2,1)S(1)} %copy-done.1, f32[2048]{0:T(1024)S(1)} %copy-done.2, f32[128]{0:T(128)S(1)} %add_rsqrt_fusion), kind=kOutput, calls=%fused_computation.34 | convolution fusion | flops 1074790400 | bytes 17834496 | tf_op jit(solution)/shard_map/dot_general | solution.py:69
  65.5 65.5 %while.10 = (s32[]{:T(128)}, f32[16]{0:T(128)S(1)}, s32[16]{0:T(128)S(1)}, bf16[128,2048]{1,0:T(8,128)(2,1)S(1)}, bf16[2048,2048]{1,0:T(8,128)(2,1)}, /*index=5*/s32[]{:T(128)}, s32[1]{0:T(128)}, s32[]{:T(128)}, s32[]{:T(128)}) while((s32[]{:T(128)}, f32[16]{0:T(128)S(1)}, s32[16]{0:T(128)S(1)}, bf16[128,2048]{1,0:T(8,128)(2,1)S(1)}, ...), condition=%wide.region_6.7_spmd, body=%wide.region_4.6_spmd.sunk | while | flops 67633160 | bytes 558255 | solution.py:51
  66.7 2.1 fusion.36
  70.8 2.1 fusion.36
  74.9 2.1 fusion.36
  79.0 2.1 fusion.36
  83.1 2.1 fusion.36
  87.2 2.1 fusion.36
  91.3 2.1 fusion.36
  95.4 2.1 fusion.36
  99.5 2.1 fusion.36
  103.6 2.1 fusion.36
  107.7 2.1 fusion.36
  111.8 2.1 fusion.36
  115.9 2.1 fusion.36
  120.0 2.1 fusion.36
  124.1 2.1 fusion.36
  128.1 2.1 fusion.36
  131.0 43.7 %psum.36 = f32[16]{0:T(128)S(1)} all-reduce(f32[16]{0:T(128)S(1)} %get-tuple-element.31), channel_id=1, replica_groups=mesh['tok'=8,'tp'=4] {'tok','tp'}, use_global_device_ids=true, to_apply=%region_7.8 | all-reduce | flops 16 | bytes 128 | tf_op jit(solution)/shard_map/psum | solution.py:52
  174.9 6.6 %fusion.13 = (f32[2048]{0:T(1024)S(1)}, f32[128]{0:T(128)S(1)}, f32[128,2048]{1,0:T(8,128)S(1)}) fusion(bf16[128,2048]{1,0:T(8,128)(2,1)S(1)} %copy-done.1, f32[128]{0:T(128)S(1)} %add_rsqrt_fusion, f32[2048]{0:T(1024)S(1)} %copy-done.2, bf16[2048,2048]{1,0:T(8,128)(2,1)} %get-tuple-element.111, bf16[128,2048]{1,0:T(8,128)(2,1)S(1)} %get-tuple-element.112, ...), kind=kOutput, calls=%fused_computation.19 | convolution fusion | flops 1076361088 | bytes 10511360 | tf_op jit(solution)/shard_map/dot_general | solution.py:57
  181.5 6.1 %psum.37 = f32[128]{0:T(128)S(1)} all-reduce(f32[128]{0:T(128)S(1)} %get-tuple-element.33), channel_id=1, replica_groups=mesh['tok'=8,'tp'=4] {'tp'}, use_global_device_ids=true, to_apply=%region_9.10 | all-reduce | flops 128 | bytes 1024 | tf_op jit(solution)/shard_map/psum | solution.py:65
  187.7 37.6 %all-reduce = (f32[2048]{0:T(1024)S(1)}, f32[2048]{0:T(1024)S(1)}) all-reduce(f32[2048]{0:T(1024)S(1)} %get-tuple-element.32, f32[2048]{0:T(1024)S(1)} %convert_reduce_fusion), channel_id=1, replica_groups=mesh['tok'=8,'tp'=4] {'tok'}, use_global_device_ids=true, to_apply=%region_11.12 | all-reduce | flops 4096 | bytes 32768 | tf_op jit(solution)/shard_map/psum | solution.py:60
  225.9 1.1 fusion.12
  227.1 122.1 %reduce-scatter.5.cloned.1.call-done = f32[2048,256]{1,0:T(8,128)} async-done(((f32[2048,2048]{1,0:T(8,128)}), f32[2048,256]{1,0:T(8,128)}) %reduce-scatter.5.cloned.1.call-update) | async-done | bytes 2097168 | tf_op jit(solution)/shard_map/reduce_scatter | solution.py:72
  349.2 3.0 multiply_multiply_fusion
  (68 shorter events, 23.2 us)
Async XLA Ops:
  7.2 15.7 %copy-start = (s32[128,16]{0,1:T(8,128)S(1)}, s32[128,16]{0,1:T(8,128)}, u32[]{:S(2)}) copy-start(s32[128,16]{0,1:T(8,128)} %param.16) | copy-start | bytes 24580
  7.2 40.9 %reduce-scatter.3.cloned.1.call-start = ((), (), s32[]{:S(2)}) async-start(), calls=%async_computation.2 | async-start | bytes 1310720 | tf_op jit(solution)/shard_map/reduce_scatter | solution.py:34
  16.9 6.2 %copy-start.5 = (f32[128,16]{0,1:T(8,128)S(1)}, f32[128,16]{0,1:T(8,128)}, u32[]{:S(2)}) copy-start(f32[128,16]{0,1:T(8,128)} %param.15) | copy-start | bytes 24580
  16.9 31.3 %copy-start.3 = (f32[2048]{0:T(1024)S(1)}, f32[2048]{0:T(1024)}, u32[]{:S(2)}) copy-start(f32[2048]{0:T(1024)} %param.13) | copy-start | bytes 24580
  16.9 32.4 %copy-start.4 = (f32[16,128]{1,0:T(8,128)S(1)}, f32[16,128]{1,0:T(8,128)}, u32[]{:S(2)}) copy-start(f32[16,128]{1,0:T(8,128)} %param.14) | copy-start | bytes 24580
  16.9 40.4 %copy-start.1 = (bf16[128,2048]{1,0:T(8,128)(2,1)S(1)}, bf16[128,2048]{1,0:T(8,128)(2,1)}, u32[]{:S(2)}) copy-start(bf16[128,2048]{1,0:T(8,128)(2,1)} %param.10) | copy-start | bytes 1572868
  16.9 40.4 %copy-start.2 = (f32[2048]{0:T(1024)S(1)}, f32[2048]{0:T(1024)}, u32[]{:S(2)}) copy-start(f32[2048]{0:T(1024)} %param.11) | copy-start | bytes 24580
  22.8 326.3 %reduce-scatter.5.cloned.1.call-start = ((), (), s32[]{:S(2)}) async-start(), calls=%async_computation.3 | async-start | bytes 18874368 | tf_op jit(solution)/shard_map/reduce_scatter | solution.py:72
  65.4 109.3 %copy-start.6 = (s32[16]{0:T(128)S(1)}, s32[16]{0:T(128)}, u32[]{:S(2)}) copy-start(s32[16]{0:T(128)} %param.17) | copy-start | bytes 196
Sparse Core Ops, SparseCore 0:
  22.9 25.1 reduce-scatter.2
  65.6 283.5 reduce-scatter.4
where the time goes:
time: 361 us; the launch traced here: 359 us
  waiting for transfers between devices  147 us (41%)
  blocking collectives  102 us (28%)
  matrix products  54.3 us (15%)
  local copies, waits for them, and re-layouts  22.1 us (6%)
  between operations  14.2 us (4%)
  loops' own time  10.5 us (3%)
  other arithmetic  8.51 us (2%)
    reduce_scatter x1, waiting for transfers between devices, per_device(): lax.psum_scatter(weight_term, 'tok', scatter_dimension=1, tiled=True)  122 us
    psum x1, blocking collectives, per_device(): squares = lax.psum(local_squares, ('tok', 'tp'))  43.7 us
    psum x1, blocking collectives, per_device(): lax.psum((jnp.sum(norm_grad * unit, axis=0), jnp.sum(grad_float, axis=0))...  37.6 us
    dot_general x16, matrix products, objective_square(): lax.dot_general(grad_slice, weight_slice, (((1,), (1,)), ((), ())), prefe...  33.5 us
    reduce_scatter x1, waiting for transfers between devices, per_device(): lax.psum_scatter(partial_value, 'tp', scatter_dimension=0, tiled=True)  24.9 us
    dynamic_update_slice x16, local copies, waits for them, and re-layouts, per_device(): local_squares = lax.map(objective_square, jnp.arange(objectives))  12.1 us
    another operation x1, loops' own time, per_device(): local_squares = lax.map(objective_square, jnp.arange(objectives))  10.5 us
    dynamic_slice x16, local copies, waits for them, and re-layouts, per_device(): local_squares = lax.map(objective_square, jnp.arange(objectives))  9.33 us
  transfers between devices with their start and end apart: 2, of which 2 were waited for; matrix products, arithmetic and copies ran while one was open for 18% of the time, Pallas kernels for 0%

commit v1 on v0

--- a/solution.py
+++ b/solution.py
@@ -49,7 +49,9 @@
         return jnp.sum(feature_grad * feature_grad)
 
     local_squares = lax.map(objective_square, jnp.arange(objectives))
-    squares = lax.psum(local_squares, ("tok", "tp"))
+    squares = local_squares
+    for axis in ("tp", "tok"):
+        squares = lax.psum(squares, axis)
     obj_rms = jnp.sqrt(squares / (total_tokens * D) + grad_eps)
     balance = obj_weight.astype(jnp.float32) / denominator / obj_rms
     balance_cols = jnp.repeat(balance, hidden)

time: 361 us -> 359 us (level)
  blocking collectives: 102 us -> 86.1 us
  waiting for transfers between devices: 147 us -> 162 us
    reduce_scatter x1, waiting for transfers between devices: 122 us -> 137 us  [per_device(): lax.psum_scatter(weight_term, 'tok', scatter_dimension=1, tiled=True)]
    psum x1 -> x2, blocking collectives: 43.7 us -> 29.3 us  [per_device(): squares = lax.psum(squares, axis)]
where the time goes in v1:
time: 359 us; the launch traced here: 358 us
  waiting for transfers between devices  162 us (45%)
  blocking collectives  86.1 us (24%)
  matrix products  54.1 us (15%)
  local copies, waits for them, and re-layouts  22.1 us (6%)
  between operations  14.2 us (4%)
  loops' own time  10.5 us (3%)
  other arithmetic  8.51 us (2%)
    reduce_scatter x1, waiting for transfers between devices, per_device(): lax.psum_scatter(weight_term, 'tok', scatter_dimension=1, tiled=True)  137 us
    psum x1, blocking collectives, per_device(): lax.psum((jnp.sum(norm_grad * unit, axis=0), jnp.sum(grad_float, axis=0))...  35.7 us
    dot_general x16, matrix products, objective_square(): lax.dot_general(grad_slice, weight_slice, (((1,), (1,)), ((), ())), prefe...  33.5 us
    psum x2, blocking collectives, per_device(): squares = lax.psum(squares, axis)  29.3 us
    reduce_scatter x1, waiting for transfers between devices, per_device(): lax.psum_scatter(partial_value, 'tp', scatter_dimension=0, tiled=True)  24.9 us
    dynamic_update_slice x16, local copies, waits for them, and re-layouts, per_device(): local_squares = lax.map(objective_square, jnp.arange(objectives))  12.1 us
    another operation x1, loops' own time, per_device(): local_squares = lax.map(objective_square, jnp.arange(objectives))  10.5 us
    dynamic_slice x16, local copies, waits for them, and re-layouts, per_device(): local_squares = lax.map(objective_square, jnp.arange(objectives))  9.33 us
  transfers between devices with their start and end apart: 2, of which 2 were waited for; matrix products, arithmetic and copies ran while one was open for 18% of the time, Pallas kernels for 0%

profile of v1, /device:TPU:0, one launch (start us, length us, event | category | flops | bytes accessed | tf_op | source)
XLA Modules:
  0.0 357.6 jit_solution(12243835203068716780)
XLA Ops:
  7.2 1.2 fusion.14
  8.5 8.4 %psum.42 = f32[128]{0:T(128)S(1)} all-reduce(f32[128]{0:T(128)S(1)} %fusion.14), channel_id=1, replica_groups=mesh['tok'=8,'tp'=4] {'tp'}, use_global_device_ids=true, to_apply=%region_1.0 | all-reduce | flops 128 | bytes 1024 | tf_op jit(solution)/shard_map/psum | solution.py:29
  16.9 5.9 %fusion.26 = f32[128,2048]{1,0:T(8,128)} fusion(bf16[2048,2048]{1,0:T(8,128)(2,1)} %param.12, bf16[128,2048]{1,0:T(8,128)(2,1)} %param.10, f32[2048]{0:T(1024)} %param.11, f32[128]{0:T(128)S(1)} %add_rsqrt_fusion), kind=kOutput, calls=%fused_computation.35 | convolution fusion | flops 1074790400 | bytes 9970176 | tf_op jit(solution)/shard_map/dot_general | solution.py:33
  23.2 24.9 %reduce-scatter.3.cloned.1.call-done = f32[32,2048]{1,0:T(8,128)} async-done(((f32[128,2048]{1,0:T(8,128)}), f32[32,2048]{1,0:T(8,128)}) %reduce-scatter.3.cloned.1.call-update) | async-done | bytes 262160 | tf_op jit(solution)/shard_map/reduce_scatter | solution.py:34
  49.5 1.1 fusion.20
  50.6 6.6 %all_gather.3 = bf16[128,2048]{1,0:T(8,128)(2,1)S(1)} all-gather(bf16[32,2048]{1,0:T(8,128)(2,1)S(1)} %fusion.20), channel_id=1, replica_groups=mesh['tok'=8,'tp'=4] {'tp'}, dimensions={0}, use_global_device_ids=true | all-gather | bytes 655360 | tf_op jit(solution)/shard_map/all_gather | solution.py:40
  57.3 8.2 %fusion.24 = f32[2048,2048]{1,0:T(8,128)} fusion(bf16[128,2048]{1,0:T(8,128)(2,1)S(1)} %all_gather.3, bf16[128,2048]{1,0:T(8,128)(2,1)S(1)} %copy-done.1, f32[2048]{0:T(1024)S(1)} %copy-done.2, f32[128]{0:T(128)S(1)} %add_rsqrt_fusion), kind=kOutput, calls=%fused_computation.34 | convolution fusion | flops 1074790400 | bytes 17834496 | tf_op jit(solution)/shard_map/dot_general | solution.py:71
  65.5 65.5 %while.10 = (s32[]{:T(128)}, f32[16]{0:T(128)S(1)}, s32[16]{0:T(128)S(1)}, bf16[128,2048]{1,0:T(8,128)(2,1)S(1)}, bf16[2048,2048]{1,0:T(8,128)(2,1)}, /*index=5*/s32[]{:T(128)}, s32[1]{0:T(128)}, s32[]{:T(128)}, s32[]{:T(128)}) while((s32[]{:T(128)}, f32[16]{0:T(128)S(1)}, s32[16]{0:T(128)S(1)}, bf16[128,2048]{1,0:T(8,128)(2,1)S(1)}, ...), condition=%wide.region_6.7_spmd, body=%wide.region_4.6_spmd.sunk | while | flops 67633160 | bytes 558255 | solution.py:51
  66.7 2.1 fusion.36
  70.8 2.1 fusion.36
  74.9 2.1 fusion.36
  79.0 2.1 fusion.36
  83.1 2.1 fusion.36
  87.2 2.1 fusion.36
  91.3 2.1 fusion.36
  95.4 2.1 fusion.36
  99.5 2.1 fusion.36
  103.6 2.1 fusion.36
  107.7 2.1 fusion.36
  111.8 2.1 fusion.36
  115.9 2.1 fusion.36
  120.0 2.1 fusion.36
  124.1 2.1 fusion.36
  128.1 2.1 fusion.36
  131.0 7.0 %psum.43 = f32[16]{0:T(128)S(1)} all-reduce(f32[16]{0:T(128)S(1)} %get-tuple-element.31), channel_id=1, replica_groups=mesh['tok'=8,'tp'=4] {'tp'}, use_global_device_ids=true, to_apply=%region_7.8 | all-reduce | flops 16 | bytes 128 | tf_op jit(solution)/shard_map/psum | solution.py:54
  138.0 22.3 %psum.44 = f32[16]{0:T(128)S(1)} all-reduce(f32[16]{0:T(128)S(1)} %psum.43), channel_id=1, replica_groups=mesh['tok'=8,'tp'=4] {'tok'}, use_global_device_ids=true, to_apply=%region_8.9 | all-reduce | flops 16 | bytes 128 | tf_op jit(solution)/shard_map/psum | solution.py:54
  160.5 6.5 %fusion.13 = (f32[2048]{0:T(1024)S(1)}, f32[128]{0:T(128)S(1)}, f32[128,2048]{1,0:T(8,128)S(1)}) fusion(bf16[128,2048]{1,0:T(8,128)(2,1)S(1)} %copy-done.1, f32[128]{0:T(128)S(1)} %add_rsqrt_fusion, f32[2048]{0:T(1024)S(1)} %copy-done.2, bf16[2048,2048]{1,0:T(8,128)(2,1)} %get-tuple-element.111, bf16[128,2048]{1,0:T(8,128)(2,1)S(1)} %get-tuple-element.112, ...), kind=kOutput, calls=%fused_computation.19 | convolution fusion | flops 1076361088 | bytes 10511360 | tf_op jit(solution)/shard_map/dot_general | solution.py:59
  167.0 6.1 %psum.45 = f32[128]{0:T(128)S(1)} all-reduce(f32[128]{0:T(128)S(1)} %get-tuple-element.33), channel_id=1, replica_groups=mesh['tok'=8,'tp'=4] {'tp'}, use_global_device_ids=true, to_apply=%region_10.11 | all-reduce | flops 128 | bytes 1024 | tf_op jit(solution)/shard_map/psum | solution.py:67
  173.2 35.7 %all-reduce = (f32[2048]{0:T(1024)S(1)}, f32[2048]{0:T(1024)S(1)}) all-reduce(f32[2048]{0:T(1024)S(1)} %get-tuple-element.32, f32[2048]{0:T(1024)S(1)} %convert_reduce_fusion), channel_id=1, replica_groups=mesh['tok'=8,'tp'=4] {'tok'}, use_global_device_ids=true, to_apply=%region_12.13 | all-reduce | flops 4096 | bytes 32768 | tf_op jit(solution)/shard_map/psum | solution.py:62
  209.5 1.1 fusion.12
  210.7 137.0 %reduce-scatter.5.cloned.1.call-done = f32[2048,256]{1,0:T(8,128)} async-done(((f32[2048,2048]{1,0:T(8,128)}), f32[2048,256]{1,0:T(8,128)}) %reduce-scatter.5.cloned.1.call-update) | async-done | bytes 2097168 | tf_op jit(solution)/shard_map/reduce_scatter | solution.py:74
  347.7 3.0 multiply_multiply_fusion
  (69 shorter events, 24.2 us)
Async XLA Ops:
  7.2 15.7 %copy-start = (s32[128,16]{0,1:T(8,128)S(1)}, s32[128,16]{0,1:T(8,128)}, u32[]{:S(2)}) copy-start(s32[128,16]{0,1:T(8,128)} %param.16) | copy-start | bytes 24580
  7.2 40.9 %reduce-scatter.3.cloned.1.call-start = ((), (), s32[]{:S(2)}) async-start(), calls=%async_computation.2 | async-start | bytes 1310720 | tf_op jit(solution)/shard_map/reduce_scatter | solution.py:34
  16.9 6.2 %copy-start.5 = (f32[128,16]{0,1:T(8,128)S(1)}, f32[128,16]{0,1:T(8,128)}, u32[]{:S(2)}) copy-start(f32[128,16]{0,1:T(8,128)} %param.15) | copy-start | bytes 24580
  16.9 31.3 %copy-start.3 = (f32[2048]{0:T(1024)S(1)}, f32[2048]{0:T(1024)}, u32[]{:S(2)}) copy-start(f32[2048]{0:T(1024)} %param.13) | copy-start | bytes 24580
  16.9 32.4 %copy-start.4 = (f32[16,128]{1,0:T(8,128)S(1)}, f32[16,128]{1,0:T(8,128)}, u32[]{:S(2)}) copy-start(f32[16,128]{1,0:T(8,128)} %param.14) | copy-start | bytes 24580
  16.9 40.4 %copy-start.1 = (bf16[128,2048]{1,0:T(8,128)(2,1)S(1)}, bf16[128,2048]{1,0:T(8,128)(2,1)}, u32[]{:S(2)}) copy-start(bf16[128,2048]{1,0:T(8,128)(2,1)} %param.10) | copy-start | bytes 1572868
  16.9 40.4 %copy-start.2 = (f32[2048]{0:T(1024)S(1)}, f32[2048]{0:T(1024)}, u32[]{:S(2)}) copy-start(f32[2048]{0:T(1024)} %param.11) | copy-start | bytes 24580
  22.8 324.9 %reduce-scatter.5.cloned.1.call-start = ((), (), s32[]{:S(2)}) async-start(), calls=%async_computation.3 | async-start | bytes 18874368 | tf_op jit(solution)/shard_map/reduce_scatter | solution.py:74
  65.4 94.9 %copy-start.6 = (s32[16]{0:T(128)S(1)}, s32[16]{0:T(128)}, u32[]{:S(2)}) copy-start(s32[16]{0:T(128)} %param.17) | copy-start | bytes 196
Sparse Core Ops, SparseCore 0:
  22.9 25.1 reduce-scatter.2
  65.6 282.0 reduce-scatter.4
